TPU v7x, 32 devices: a whole 2x2x4 slice. The times are simulated.
32 devices in a mesh: date: 8 (over z, x), az: 4 (over y, core).
Axes of the slice: x: 2, y: 2, z: 4, core: 2. Of those that a mesh axis runs over, the one named last changes fastest.
Arguments:
- slc: float32 [48, 2, 32, 1024], P('date', None, 'az'), may hold values from -12 to 12
- pairs: int32 [2, 512, 2], replicated, may hold values from 0 to 47, as said below
Outputs:
- interferogram: float32 [2, 512, 2, 8, 64], P(None, 'date', None, 'az')
- coherence: float32 [2, 512, 8, 64], P(None, 'date', 'az')
Inputs may be any that keep to these rules, and one draw needn't show every extreme that they name: In each round the two dates of a pair differ; the pairs in the block of 64 rows of one device name exactly 8 distinct dates, and at most 2 distinct dates out of any one block of 6 dates, exactly 2 out of some block.
All inputs are finite; a program needn't handle non-finite values.
Results may differ from a plain program's by a relative error of at most 0.0014.
Values may be sent and summed in bfloat16 or wider, within the bound.
A program may use at most 64 MiB of HBM per device.

v0:
```python
import jax
import jax.numpy as jnp
from jax import lax
from jax.experimental import pallas as pl
from jax.experimental.pallas import tpu as pltpu
from jax.sharding import PartitionSpec as P

CAP = 2


def with_halo(shard, sides, width):
    for axis, dim in sides:
        peers, length = (lax.axis_size(axis), shard.shape[dim])
        up = [(i, (i + 1) % peers) for i in range(peers - 1)]
        down = [(j, i) for i, j in up]
        last = lax.slice_in_dim(shard, length - width, length, axis=dim)
        first = lax.slice_in_dim(shard, 0, width, axis=dim)
        before = lax.ppermute(last, axis, up)
        after = lax.ppermute(first, axis, down)
        shard = jnp.concatenate([before, shard, after], axis=dim)
    return shard


def multilook(field):
    shape = field.shape
    blocks = field.reshape(shape[:-2] + (shape[-2] // 4, 4, shape[-1] // 16, 16))
    return blocks.mean(axis=(-3, -1))


def pair_looks(tiles):
    first = tiles[:, 0].astype(jnp.float32)
    second = tiles[:, 1].astype(jnp.float32)
    first_re, first_im = (first[:, 0], first[:, 1])
    second_re, second_im = (second[:, 0], second[:, 1])
    prod_re = first_re * second_re + first_im * second_im
    prod_im = first_im * second_re - first_re * second_im
    power_a = first_re * first_re + first_im * first_im
    power_b = second_re * second_re + second_im * second_im
    return jnp.stack(
        [multilook(prod_re), multilook(prod_im), multilook(power_a), multilook(power_b)], axis=1
    )


def coherence_from(padded):
    lines = padded.shape[-2] - 4
    columns = padded.shape[-1]
    az_sum = padded[..., 0:lines, :]
    for offset in range(1, 5):
        az_sum = az_sum + padded[..., offset : offset + lines, :]
    widths = [(0, 0)] * (az_sum.ndim - 1) + [(2, 2)]
    wide = jnp.pad(az_sum, widths)
    boxed = wide[..., 0:columns]
    for offset in range(1, 5):
        boxed = boxed + wide[..., offset : offset + columns]
    numer = jnp.sqrt(boxed[..., 0, :, :] ** 2 + boxed[..., 1, :, :] ** 2)
    return numer / jnp.sqrt(boxed[..., 2, :, :] * boxed[..., 3, :, :])


def per_device_general(slc, pairs):
    date_count = lax.axis_size("date")
    own_index = lax.axis_index("date")
    date_dev = slc.shape[0]
    pair_dev = pairs.shape[1] // date_count
    tile_shape = slc.shape[1:]
    quantized = lax.optimization_barrier(slc.astype(jnp.bfloat16))
    all_ids = jnp.arange(date_count * date_dev, dtype=jnp.int32)
    local_ids = own_index * date_dev + jnp.arange(date_dev, dtype=jnp.int32)
    local_pos = jnp.arange(date_dev, dtype=jnp.int32)
    slot_ids = jnp.arange(CAP, dtype=jnp.int32)
    looks_list = []
    for round_index in range(pairs.shape[0]):
        block = pairs[round_index]
        own_pairs = lax.dynamic_slice_in_dim(block, own_index * pair_dev, pair_dev, 0)
        entries = own_pairs.reshape(-1)
        wanted = block.reshape(date_count, 2 * pair_dev)
        needed = jnp.any(wanted[:, :, None] == local_ids[None, None, :], axis=1).astype(jnp.int32)
        ranks = jnp.cumsum(needed, axis=1) - needed
        picked = needed[:, None, :] * (ranks[:, None, :] == slot_ids[None, :, None]).astype(
            jnp.int32
        )
        source_local = jnp.sum(picked * local_pos[None, None, :], axis=2)
        present = jnp.sum(picked, axis=2) > 0
        outgoing = jnp.take(quantized, source_local.reshape(-1), axis=0).reshape(
            (date_count, CAP) + tile_shape
        )
        outgoing = jnp.where(present[:, :, None, None, None], outgoing, jnp.zeros((), jnp.bfloat16))
        incoming = lax.all_to_all(outgoing, "date", split_axis=0, concat_axis=0, tiled=True)
        matches = entries[:, None] == all_ids[None, :]
        my_need = jnp.any(matches, axis=0).astype(jnp.int32).reshape(date_count, date_dev)
        my_rank = (jnp.cumsum(my_need, axis=1) - my_need).reshape(-1)
        entry_slot = jnp.sum(jnp.where(matches, my_rank[None, :], 0), axis=1)
        position = entries // date_dev * CAP + entry_slot
        fetched = jnp.take(incoming.reshape((date_count * CAP,) + tile_shape), position, axis=0)
        looks = pair_looks(fetched.reshape((pair_dev, 2) + tile_shape))
        looks_list.append(looks)
    stacked = jnp.stack(looks_list, axis=0)
    padded = with_halo(stacked, (("az", 3),), 2)
    coherence = coherence_from(padded)
    interferogram = stacked[:, :, 0:2]
    return (interferogram, coherence)


LINES, SAMPLES = 4, 16
STEPS = ((0, 2, 2), (0, 2, 1), (1, 8, 8), (1, 8, 4), (1, 8, 2), (1, 8, 1))


def iota(shape, dim):
    return lax.broadcasted_iota(jnp.int32, shape, dim)


def place_of(leaf):
    bit = [(leaf >> n) & 1 for n in range(6)]
    return 32 * bit[3] + 16 * bit[4] + 8 * bit[5] + 4 * bit[0] + 2 * bit[1] + bit[2]


def rolled(x, shift, dim):
    return pltpu.roll(x, shift % x.shape[dim], dim)


def join(one, two, dim, unit, dist, phase):
    low = ((iota(one.shape, dim) - unit * phase) & (unit * dist)) == 0
    kept = jnp.where(low, one, two)
    other = jnp.where(low, two, one)
    return kept + rolled(other, -unit * dist, dim)


def cell_sums(real, imag):
    count = len(real)
    couples = [(i, j) for i in range(count) for j in range(i + 1, count)]

    def quantity(place):
        if place < len(couples):
            i, j = couples[place]
            return real[i] * real[j] + imag[i] * imag[j]
        place -= len(couples)
        if place < len(couples):
            i, j = couples[place]
            return imag[i] * real[j] - real[i] * imag[j]
        i = place - len(couples)
        return real[i] * real[i] + imag[i] * imag[i]

    def build(level, base, phases):
        if level == 0:
            return quantity(place_of(base))
        dim, unit, dist = STEPS[level - 1]
        moved = tuple(p + dist if d == dim else p for d, p in enumerate(phases))
        one = build(level - 1, base, phases)
        two = build(level - 1, base + (1 << (level - 1)), moved)
        return join(one, two, dim, unit, dist, phases[dim])

    return build(len(STEPS), 0, (0, 0))


def in_three(x):
    parts = []
    for _ in range(3):
        part = x.astype(jnp.bfloat16)
        parts.append(part)
        x = x - part.astype(jnp.float32)
    return jnp.concatenate(parts, 0)


def sample_order():
    src, dst = iota((128, 128), 0), iota((128, 128), 1)
    hit = dst == (src % SAMPLES) * (128 // SAMPLES) + src // SAMPLES
    return jnp.where(hit, 1.0 / 8, 0.0).astype(jnp.bfloat16)


def table_of(tiles):
    lane, sub = iota((8, 128), 1), iota((8, 128), 0)
    tiles = list(tiles)
    for b in range(3):
        dist = 8 << b
        low = (lane & dist) == 0
        for j in range(8):
            if not j >> b & 1:
                one, two = tiles[j], tiles[j | 1 << b]
                tiles[j] = jnp.where(low, one, rolled(two, dist, 1))
                tiles[j | 1 << b] = jnp.where(low, rolled(one, -dist, 1), two)
    even, first = (sub & 1) == 0, lane < 64
    out = []
    for tile in tiles:
        far = rolled(tile, 64, 1)
        moved = jnp.where(even, rolled(far, -1, 0), rolled(far, 1, 0))
        out.append(jnp.where(even == first, tile, moved))
    return out


def box_of(own, before, after):
    lane = iota(own.shape, 1)
    first = lane < 64
    both = own + rolled(own, 64, 1)
    both = both + jnp.where(first, before + rolled(before, 64, 1), before)
    both = both + jnp.where(first, after, after + rolled(after, 64, 1))
    cell = lane & 63
    out = both
    for o in (-2, -1, 1, 2):
        valid = (cell + o >= 0) & (cell + o < 64)
        out = out + jnp.where(valid, rolled(both, -o, 1), 0.0)
    return out


def pick(places, values):
    return jnp.where(iota((192, 128), 0) & 63 == places, values, 0.0)


def picks(rank_a, rank_b, count):
    first = iota(rank_a.shape, 1) < 64
    low, high = jnp.minimum(rank_a, rank_b), jnp.maximum(rank_a, rank_b)
    couples = count * (count - 1) // 2
    place = ((low * (2 * count - 1 - low)) >> 1) + high - low - 1
    sign = jnp.where(first | (rank_a < rank_b), 1.0, -1.0)
    products = pick(place + jnp.where(first, 0, couples), sign)
    powers = pick(2 * couples + jnp.where(first, rank_a, rank_b), jnp.ones_like(sign))
    return products, powers


MESH = pl.DeviceIdType.MESH


def list_dates(pairs, dates, peers):
    length = pairs.shape[1]
    part = length // peers
    date = iota((dates, length), 0)
    named = (pairs[0:1] == date) | (pairs[1:2] == date)
    parts = iota((length, 128), 0) // part == iota((length, 128), 1)
    dims = (((1,), (0,)), ((), ()))
    one = jnp.bfloat16
    counts = lax.dot_general(
        named.astype(jnp.float32).astype(one),
        parts.astype(jnp.float32).astype(one),
        dims,
        preferred_element_type=jnp.float32,
    )
    needed = counts > 0.5
    before = iota((dates, dates), 1) < iota((dates, dates), 0)
    rank = lax.dot_general(
        before.astype(jnp.float32).astype(one),
        needed.astype(jnp.float32).astype(one),
        dims,
        preferred_element_type=jnp.float32,
    )
    rank = jnp.where(needed, rank, -1.0).astype(jnp.int32)
    date = iota(rank.shape, 0)
    rows = [jnp.sum(jnp.where(rank == k, date, 0), axis=0, keepdims=True) for k in range(peers)]
    return jnp.concatenate(rows, 0)


def stack_kernel(
    slc_ref,
    pairs_ref,
    table,
    boxed_ref,
    chosen,
    lines,
    sent,
    held,
    full,
    sums,
    tiles,
    halo,
    listed,
    ids,
    line_sem,
    send_a,
    recv_a,
    send_b,
    recv_b,
    send_h,
    recv_h,
    list_sem,
):
    peers, az_size = lax.axis_size("date"), lax.axis_size("az")
    me, az = lax.axis_index("date"), lax.axis_index("az")
    date_dev = slc_ref.shape[0]
    rounds = pairs_ref.shape[0]
    width = slc_ref.shape[3] // peers
    images_dev = 2 * date_dev
    sides = ((-1, az > 0), (1, az < az_size - 1))

    barrier = pltpu.get_barrier_semaphore()
    for o in range(1, peers):
        pl.semaphore_signal(
            barrier, inc=1, device_id={"date": lax.rem(me + o, peers)}, device_id_type=MESH
        )
    for step, there in sides:

        @pl.when(there)
        def _():
            pl.semaphore_signal(barrier, inc=1, device_id={"az": az + step}, device_id_type=MESH)

    def line(n):
        return pltpu.make_async_copy(slc_ref.at[n], lines.at[n], line_sem.at[n])

    for n in range(date_dev):
        line(n).start()
    rows_date = sent.shape[1] // date_dev
    for n in range(date_dev):
        line(n).wait()
        for j in range(peers):
            part = lines[n, :, :, j * width : (j + 1) * width]
            at = slice(n * rows_date, (n + 1) * rows_date)
            sent[j, at] = part.reshape(rows_date, width).astype(jnp.bfloat16)
    greeted = peers - 1 + (az > 0).astype(jnp.int32) + (az < az_size - 1).astype(jnp.int32)
    pl.semaphore_wait(barrier, greeted)

    def images(o):
        peer = lax.rem(me + o, peers)
        return pltpu.make_async_remote_copy(
            src_ref=sent.at[peer],
            dst_ref=held.at[me],
            send_sem=send_a.at[o],
            recv_sem=recv_a.at[o],
            device_id={"date": peer},
            device_id_type=MESH,
        )

    for o in range(1, peers):
        images(o).start()
    for r in range(rounds):
        listed[r * peers : (r + 1) * peers, :] = list_dates(
            pairs_ref[r], date_dev * peers, peers
        )
    fetch = pltpu.make_async_copy(listed, ids, list_sem)
    fetch.start()
    order = sample_order()

    def take(owner, block):
        spread = jnp.dot(block, order, preferred_element_type=jnp.float32)
        for image in range(images_dev):
            for group in range(2):
                row = image * 8 + group * LINES
                at = (owner * images_dev + image, pl.ds(group, LINES, stride=2))
                full[at] = spread[row : row + LINES]

    take(me, sent[me])
    fetch.wait()
    lane = iota((1, 128), 1)
    for r in range(rounds):
        ranks = []
        for c in range(2):
            start = pl.multiple_of(me // 2 * 128, 128)
            near = pairs_ref[r, c : c + 1, pl.ds(start, 128)]
            own = jnp.where((lane < 64) == (lax.rem(me, 2) == 0), near, rolled(near, 64, 1))
            rank = jnp.zeros_like(own)
            for k in range(peers):
                rank = rank + (own > ids[r * peers + k, me]).astype(jnp.int32)
            ranks.append(rank)
        products, powers = picks(*ranks, peers)
        chosen[r, :128, :] = products.T.astype(jnp.bfloat16)
        chosen[r, 128:, :] = powers.T.astype(jnp.bfloat16)
    for o in range(1, peers):
        images(o).wait_recv()
        owner = lax.rem(me + peers - o, peers)
        take(owner, held[owner])

    def results(o):
        peer = lax.rem(me + o, peers)
        return pltpu.make_async_remote_copy(
            src_ref=sums.at[peer],
            dst_ref=tiles.at[me],
            send_sem=send_b.at[o],
            recv_sem=recv_b.at[o],
            device_id={"date": peer},
            device_id_type=MESH,
        )

    def serve(o, carry):
        peer = lax.rem(me + o, peers)
        for r in range(rounds):
            real, imag = [], []
            for k in range(peers):
                date = ids[r * peers + k, peer]
                real.append(full[2 * date])
                imag.append(full[2 * date + 1])
            sums[peer, r] = cell_sums(real, imag)

        @pl.when(o < peers)
        def _():
            results(o).start()

        return carry

    lax.fori_loop(1, peers + 1, serve, 0)
    tiles[me] = sums[me]
    for o in range(1, peers):
        results(o).wait_recv()
    for r in range(rounds):
        for k, tile in enumerate(table_of([tiles[j, r] for j in range(peers)])):
            table[r, 8 * k : 8 * k + 8, :] = tile

    def edge(n, step):
        return pltpu.make_async_remote_copy(
            src_ref=table,
            dst_ref=halo.at[n],
            send_sem=send_h.at[n],
            recv_sem=recv_h.at[n],
            device_id={"az": az + step},
            device_id_type=MESH,
        )

    for n, (step, there) in enumerate(sides):

        @pl.when(there)
        def _():
            edge(n, step).start()

        @pl.when(jnp.logical_not(there))
        def _():
            halo[1 - n] = jnp.zeros_like(halo[1 - n])

    for n, (step, there) in enumerate(sides):

        @pl.when(there)
        def _():
            edge(1 - n, step).wait_recv()

    for r in range(rounds):
        boxed_ref[r] = box_of(table[r], halo[1, r], halo[0, r])

    for o in range(1, peers):
        images(o).wait_send()
        results(o).wait_send()
    for n, (step, there) in enumerate(sides):

        @pl.when(there)
        def _():
            edge(n, step).wait_send()


def pairs_kernel(table_ref, boxed_ref, chosen_ref, ifg_ref, coh_ref):
    for r in range(table_ref.shape[0]):
        means = jnp.dot(
            chosen_ref[r, :128, :], in_three(table_ref[r]), preferred_element_type=jnp.float32
        )
        for c in range(2):
            for row in range(2):
                part = means[64 * c : 64 * c + 64, 64 * row : 64 * row + 64]
                ifg_ref[pl.ds(256 * r + 2 * c + row, 64, stride=4), :] = part
        parts = jnp.dot(
            chosen_ref[r], in_three(boxed_ref[r]), preferred_element_type=jnp.float32
        )
        size = jnp.sqrt(parts[:64] * parts[:64] + parts[64:128] * parts[64:128])
        coherence = size / jnp.sqrt(parts[128:192] * parts[192:])
        for row in range(2):
            part = coherence[:, 64 * row : 64 * row + 64]
            coh_ref[pl.ds(128 * r + row, 64, stride=2), :] = part


def per_device_few(slc, pairs):
    peers = lax.axis_size("date")
    rounds = pairs.shape[0]
    pair_dev = pairs.shape[1] // peers
    date_dev, _, lines, columns = slc.shape
    width = columns // peers
    rows = date_dev * 2 * lines
    cells = columns // SAMPLES
    vmem = pl.BlockSpec(memory_space=pltpu.VMEM)
    dma = pltpu.SemaphoreType.DMA
    found = pl.pallas_call(
        stack_kernel,
        out_shape=(
            jax.ShapeDtypeStruct((rounds, 64, 128), jnp.float32),
            jax.ShapeDtypeStruct((rounds, 64, 128), jnp.float32),
            jax.ShapeDtypeStruct((rounds, 256, 192), jnp.bfloat16),
        ),
        in_specs=[pl.BlockSpec(memory_space=pl.ANY), vmem],
        out_specs=(vmem,) * 3,
        scratch_shapes=[
            pltpu.VMEM(slc.shape, jnp.float32),
            pltpu.VMEM((peers, rows, width), jnp.bfloat16),
            pltpu.VMEM((peers, rows, width), jnp.bfloat16),
            pltpu.VMEM((peers * date_dev * 2, lines, width), jnp.float32),
            pltpu.VMEM((peers, rounds, 8, 128), jnp.float32),
            pltpu.VMEM((peers, rounds, 8, 128), jnp.float32),
            pltpu.VMEM((2, rounds, 64, 128), jnp.float32),
            pltpu.VMEM((rounds * peers, 128), jnp.int32),
            pltpu.SMEM((rounds * peers, 128), jnp.int32),
            dma((date_dev,)),
            dma((peers,)),
            dma((peers,)),
            dma((peers,)),
            dma((peers,)),
            dma((2,)),
            dma((2,)),
            dma,
        ],
        compiler_params=pltpu.CompilerParams(collective_id=0, has_side_effects=True),
    )(slc, pairs.transpose(0, 2, 1))
    ifg, coh = pl.pallas_call(
        pairs_kernel,
        out_shape=(
            jax.ShapeDtypeStruct((rounds * pair_dev * 2 * lines // LINES, cells), jnp.float32),
            jax.ShapeDtypeStruct((rounds * pair_dev * lines // LINES, cells), jnp.float32),
        ),
        in_specs=[vmem] * 3,
        out_specs=(vmem, vmem),
    )(*found)
    return (
        ifg.reshape(rounds, pair_dev, 2, lines // LINES, cells),
        coh.reshape(rounds, pair_dev, lines // LINES, cells),
    )


def per_device(slc, pairs):
    peers = lax.axis_size("date")
    lines, columns = slc.shape[2:]
    pair_dev = pairs.shape[1] // peers
    few = (peers, pair_dev, lines, columns) == (8, 64, 2 * LINES, 64 * SAMPLES)
    return per_device_few(slc, pairs) if few else per_device_general(slc, pairs)


def solution(mesh):
    return jax.shard_map(
        per_device,
        mesh=mesh,
        in_specs=(P("date", None, "az", None), P()),
        out_specs=(P(None, "date", None, "az", None), P(None, "date", "az", None)),
        check_vma=False,
    )
```

profile of v0, /device:TPU:1, one launch (start us, length us, event | category | flops | bytes accessed | tf_op | source)
XLA Modules:
  0.0 25.1 jit_solution(11694071841325722042)
XLA Ops:
  0.6 22.5 %shard_map.41 = (f32[2,64,128]{2,1,0:T(8,128)}, f32[2,64,128]{2,1,0:T(8,128)}, bf16[2,256,192]{2,1,0:T(8,128)(2,1)}) custom-call(f32[6,2,8,1024]{3,2,1,0:T(8,128)} %slc_ref.1, s32[2,2,512]{2,1,0:T(2,128)} %bitcast.3), custom_call_target="tpu_custom_call" | custom-call | tf_op jit(solution)/shard_map/pallas_call | solution.py:460
  23.1 2.0 %shard_map.42 = (f32[512,64]{1,0:T(8,128)}, f32[256,64]{1,0:T(8,128)}) custom-call(f32[2,64,128]{2,1,0:T(8,128)} %get-tuple-element.7.table_ref, f32[2,64,128]{2,1,0:T(8,128)} %get-tuple-element.8.boxed_ref, bf16[2,256,192]{2,1,0:T(8,128)(2,1)} %get-tuple-element.9.chosen_ref), custom_call_target="tpu_custom_call" | custom-call | tf_op jit(solution)/shard_map/pallas_call | solution.py:490
where the time goes:
time: 25.4 us; the launch traced here: 25.1 us
  Pallas kernels  24.5 us (96%)
  between operations  0.64 us (3%)
    pallas_call x1, Pallas kernels, per_device_few(): pl.pallas_call(stack_kernel, out_shape=(jax.ShapeDtypeStruct((rounds, 64,...  22.5 us
    pallas_call x1, Pallas kernels, per_device_few(): pl.pallas_call(pairs_kernel, out_shape=(jax.ShapeDtypeStruct((rounds * pa...  2.03 us

commit v1 on v0

--- a/solution.py
+++ b/solution.py
@@ -6,6 +6,7 @@
 from jax.sharding import PartitionSpec as P
 
 CAP = 2
+VMEM_LIMIT = 4 << 20
 
 
 def with_halo(shard, sides, width):
@@ -248,7 +249,7 @@
 
 def stack_kernel(
     slc_ref,
-    pairs_ref,
+    pairs_hbm,
     table,
     boxed_ref,
     chosen,
@@ -261,6 +262,8 @@
     halo,
     listed,
     ids,
+    pairs_ref,
+    pairs_sem,
     line_sem,
     send_a,
     recv_a,
@@ -278,7 +281,11 @@
     images_dev = 2 * date_dev
     sides = ((-1, az > 0), (1, az < az_size - 1))
 
+    named = pltpu.make_async_copy(pairs_hbm, pairs_ref, pairs_sem)
     barrier = pltpu.get_barrier_semaphore()
+    for n in range(date_dev):
+        pltpu.make_async_copy(slc_ref.at[n], lines.at[n], line_sem).start()
+    named.start()
     for o in range(1, peers):
         pl.semaphore_signal(
             barrier, inc=1, device_id={"date": lax.rem(me + o, peers)}, device_id_type=MESH
@@ -289,14 +296,9 @@
         def _():
             pl.semaphore_signal(barrier, inc=1, device_id={"az": az + step}, device_id_type=MESH)
 
-    def line(n):
-        return pltpu.make_async_copy(slc_ref.at[n], lines.at[n], line_sem.at[n])
-
+    rows_date = sent.shape[1] // date_dev
+    pltpu.make_async_copy(slc_ref, lines, line_sem).wait()
     for n in range(date_dev):
-        line(n).start()
-    rows_date = sent.shape[1] // date_dev
-    for n in range(date_dev):
-        line(n).wait()
         for j in range(peers):
             part = lines[n, :, :, j * width : (j + 1) * width]
             at = slice(n * rows_date, (n + 1) * rows_date)
@@ -309,7 +311,7 @@
         return pltpu.make_async_remote_copy(
             src_ref=sent.at[peer],
             dst_ref=held.at[me],
-            send_sem=send_a.at[o],
+            send_sem=send_a,
             recv_sem=recv_a.at[o],
             device_id={"date": peer},
             device_id_type=MESH,
@@ -317,6 +319,7 @@
 
     for o in range(1, peers):
         images(o).start()
+    named.wait()
     for r in range(rounds):
         listed[r * peers : (r + 1) * peers, :] = list_dates(
             pairs_ref[r], date_dev * peers, peers
@@ -359,8 +362,8 @@
         return pltpu.make_async_remote_copy(
             src_ref=sums.at[peer],
             dst_ref=tiles.at[me],
-            send_sem=send_b.at[o],
-            recv_sem=recv_b.at[o],
+            send_sem=send_b,
+            recv_sem=recv_b,
             device_id={"date": peer},
             device_id_type=MESH,
         )
@@ -383,8 +386,19 @@
 
     lax.fori_loop(1, peers + 1, serve, 0)
     tiles[me] = sums[me]
-    for o in range(1, peers):
-        results(o).wait_recv()
+    others = pl.ds(0, peers - 1)
+
+    def all_of(src, dst, send_sem, recv_sem):
+        return pltpu.make_async_remote_copy(
+            src_ref=src.at[others],
+            dst_ref=dst.at[others],
+            send_sem=send_sem,
+            recv_sem=recv_sem,
+            device_id={"date": lax.rem(me + 1, peers)},
+            device_id_type=MESH,
+        )
+
+    all_of(sums, tiles, send_b, recv_b).wait_recv()
     for r in range(rounds):
         for k, tile in enumerate(table_of([tiles[j, r] for j in range(peers)])):
             table[r, 8 * k : 8 * k + 8, :] = tile
@@ -418,9 +432,8 @@
     for r in range(rounds):
         boxed_ref[r] = box_of(table[r], halo[1, r], halo[0, r])
 
-    for o in range(1, peers):
-        images(o).wait_send()
-        results(o).wait_send()
+    all_of(sent, held, send_a, recv_a.at[0]).wait_send()
+    all_of(sums, tiles, send_b, recv_b).wait_send()
     for n, (step, there) in enumerate(sides):
 
         @pl.when(there)
@@ -428,8 +441,15 @@
             edge(n, step).wait_send()
 
 
-def pairs_kernel(table_ref, boxed_ref, chosen_ref, ifg_ref, coh_ref):
-    for r in range(table_ref.shape[0]):
+def pairs_kernel(table_ref, boxed_ref, chosen_ref, ifg_hbm, coh_hbm, ifg_ref, coh_ref, sems):
+    rounds = table_ref.shape[0]
+
+    def out(r, src, dst, n):
+        rows = src.shape[0] // rounds
+        at = pl.ds(rows * r, rows)
+        return pltpu.make_async_copy(src.at[at], dst.at[at], sems.at[n, r])
+
+    for r in range(rounds):
         means = jnp.dot(
             chosen_ref[r, :128, :], in_three(table_ref[r]), preferred_element_type=jnp.float32
         )
@@ -437,6 +457,7 @@
             for row in range(2):
                 part = means[64 * c : 64 * c + 64, 64 * row : 64 * row + 64]
                 ifg_ref[pl.ds(256 * r + 2 * c + row, 64, stride=4), :] = part
+        out(r, ifg_ref, ifg_hbm, 0).start()
         parts = jnp.dot(
             chosen_ref[r], in_three(boxed_ref[r]), preferred_element_type=jnp.float32
         )
@@ -445,6 +466,10 @@
         for row in range(2):
             part = coherence[:, 64 * row : 64 * row + 64]
             coh_ref[pl.ds(128 * r + row, 64, stride=2), :] = part
+        out(r, coh_ref, coh_hbm, 1).start()
+    for r in range(rounds):
+        out(r, ifg_ref, ifg_hbm, 0).wait()
+        out(r, coh_ref, coh_hbm, 1).wait()
 
 
 def per_device_few(slc, pairs):
@@ -456,6 +481,7 @@
     rows = date_dev * 2 * lines
     cells = columns // SAMPLES
     vmem = pl.BlockSpec(memory_space=pltpu.VMEM)
+    hbm = pl.BlockSpec(memory_space=pltpu.HBM)
     dma = pltpu.SemaphoreType.DMA
     found = pl.pallas_call(
         stack_kernel,
@@ -464,7 +490,7 @@
             jax.ShapeDtypeStruct((rounds, 64, 128), jnp.float32),
             jax.ShapeDtypeStruct((rounds, 256, 192), jnp.bfloat16),
         ),
-        in_specs=[pl.BlockSpec(memory_space=pl.ANY), vmem],
+        in_specs=[hbm, hbm],
         out_specs=(vmem,) * 3,
         scratch_shapes=[
             pltpu.VMEM(slc.shape, jnp.float32),
@@ -476,25 +502,40 @@
             pltpu.VMEM((2, rounds, 64, 128), jnp.float32),
             pltpu.VMEM((rounds * peers, 128), jnp.int32),
             pltpu.SMEM((rounds * peers, 128), jnp.int32),
-            dma((date_dev,)),
+            pltpu.VMEM((rounds, 2, pairs.shape[1]), jnp.int32),
+            dma,
+            dma,
+            dma,
             dma((peers,)),
-            dma((peers,)),
-            dma((peers,)),
-            dma((peers,)),
+            dma,
+            dma,
             dma((2,)),
             dma((2,)),
             dma,
         ],
-        compiler_params=pltpu.CompilerParams(collective_id=0, has_side_effects=True),
-    )(slc, pairs.transpose(0, 2, 1))
+        compiler_params=pltpu.CompilerParams(
+            collective_id=0, has_side_effects=True, vmem_limit_bytes=VMEM_LIMIT
+        ),
+    )(
+        pltpu.with_memory_space_constraint(slc, pltpu.HBM),
+        pltpu.with_memory_space_constraint(pairs.transpose(0, 2, 1), pltpu.HBM),
+    )
+    ifg_shape = (rounds * pair_dev * 2 * lines // LINES, cells)
+    coh_shape = (rounds * pair_dev * lines // LINES, cells)
     ifg, coh = pl.pallas_call(
         pairs_kernel,
         out_shape=(
-            jax.ShapeDtypeStruct((rounds * pair_dev * 2 * lines // LINES, cells), jnp.float32),
-            jax.ShapeDtypeStruct((rounds * pair_dev * lines // LINES, cells), jnp.float32),
+            jax.ShapeDtypeStruct(ifg_shape, jnp.float32),
+            jax.ShapeDtypeStruct(coh_shape, jnp.float32),
         ),
         in_specs=[vmem] * 3,
-        out_specs=(vmem, vmem),
+        out_specs=(hbm, hbm),
+        scratch_shapes=[
+            pltpu.VMEM(ifg_shape, jnp.float32),
+            pltpu.VMEM(coh_shape, jnp.float32),
+            dma((2, rounds)),
+        ],
+        compiler_params=pltpu.CompilerParams(vmem_limit_bytes=VMEM_LIMIT),
     )(*found)
     return (
         ifg.reshape(rounds, pair_dev, 2, lines // LINES, cells),

time: 25.4 us -> 22.7 us (0.89)
  Pallas kernels: 24.5 us -> 21.9 us
    pallas_call x1, Pallas kernels: 22.5 us -> 20.8 us  [per_device_few(): pl.pallas_call(stack_kernel, out_shape=(jax.ShapeDtypeStruct((rounds, 64,...]
    pallas_call x1, Pallas kernels: 2.03 us -> 1.08 us  [per_device_few(): pl.pallas_call(pairs_kernel, out_shape=(jax.ShapeDtypeStruct(ifg_shape, j...]
where the time goes in v1:
time: 22.7 us; the launch traced here: 22.5 us
  Pallas kernels  21.9 us (96%)
  between operations  0.64 us (3%)
    pallas_call x1, Pallas kernels, per_device_few(): pl.pallas_call(stack_kernel, out_shape=(jax.ShapeDtypeStruct((rounds, 64,...  20.8 us
    pallas_call x1, Pallas kernels, per_device_few(): pl.pallas_call(pairs_kernel, out_shape=(jax.ShapeDtypeStruct(ifg_shape, j...  1.08 us

profile of v1, /device:TPU:1, one launch (start us, length us, event | category | flops | bytes accessed | tf_op | source)
XLA Modules:
  0.0 22.5 jit_solution(10959662616485803734)
XLA Ops:
  0.6 20.8 %shard_map.41 = (f32[2,64,128]{2,1,0:T(8,128)S(1)}, f32[2,64,128]{2,1,0:T(8,128)S(1)}, bf16[2,256,192]{2,1,0:T(8,128)(2,1)S(1)}) custom-call(f32[6,2,8,1024]{3,2,1,0:T(8,128)} %slc_ref.1, s32[2,2,512]{2,1,0:T(2,128)} %bitcast.3), custom_call_target="tpu_custom_call" | custom-call | tf_op jit(solution)/shard_map/pallas_call | solution.py:486
  21.4 1.1 %shard_map.42 = (f32[512,64]{1,0:T(8,128)}, f32[256,64]{1,0:T(8,128)}) custom-call(f32[2,64,128]{2,1,0:T(8,128)S(1)} %get-tuple-element.7.table_ref, f32[2,64,128]{2,1,0:T(8,128)S(1)} %get-tuple-element.8.boxed_ref, bf16[2,256,192]{2,1,0:T(8,128)(2,1)S(1)} %get-tuple-element.9.chosen_ref), custom_call_target="tpu_custom_call" | custom-call | tf_op jit(solution)/shard_map/pallas_call | solution.py:525

commit v2 on v1

--- a/solution.py
+++ b/solution.py
@@ -152,13 +152,10 @@
     return build(len(STEPS), 0, (0, 0))
 
 
-def in_three(x):
-    parts = []
-    for _ in range(3):
-        part = x.astype(jnp.bfloat16)
-        parts.append(part)
-        x = x - part.astype(jnp.float32)
-    return jnp.concatenate(parts, 0)
+def in_two(x):
+    high = x.astype(jnp.bfloat16)
+    low = (x - high.astype(jnp.float32)).astype(jnp.bfloat16)
+    return jnp.concatenate([high, low], 0)
 
 
 def sample_order():
@@ -187,13 +184,19 @@
     return out
 
 
-def box_of(own, before, after):
-    lane = iota(own.shape, 1)
-    first = lane < 64
-    both = own + rolled(own, 64, 1)
-    both = both + jnp.where(first, before + rolled(before, 64, 1), before)
-    both = both + jnp.where(first, after, after + rolled(after, 64, 1))
-    cell = lane & 63
+def both_rows(x):
+    odd = (iota(x.shape, 0) & 1) == 1
+    return x + jnp.where(odd, rolled(x, 1, 0), rolled(x, -1, 0))
+
+
+def shares_of(x):
+    odd = (iota(x.shape, 0) & 1) == 1
+    both = both_rows(x)
+    return x, jnp.where(odd, both, x), jnp.where(odd, x, both)
+
+
+def box_of(both):
+    cell = iota(both.shape, 1) & 63
     out = both
     for o in (-2, -1, 1, 2):
         valid = (cell + o >= 0) & (cell + o < 64)
@@ -202,7 +205,7 @@
 
 
 def pick(places, values):
-    return jnp.where(iota((192, 128), 0) & 63 == places, values, 0.0)
+    return jnp.where(iota((128, 128), 0) & 63 == places, values, 0.0)
 
 
 def picks(rank_a, rank_b, count):
@@ -217,6 +220,14 @@
 
 
 MESH = pl.DeviceIdType.MESH
+
+
+def partner(me, m):
+    out = 0
+    for n in range(3):
+        mine, other = me // 2**n % 2, m // 2**n % 2
+        out = out + 2**n * (mine + other - 2 * mine * other)
+    return out
 
 
 def list_dates(pairs, dates, peers):
@@ -259,7 +270,8 @@
     full,
     sums,
     tiles,
-    halo,
+    near_sums,
+    near_tiles,
     listed,
     ids,
     pairs_ref,
@@ -269,8 +281,6 @@
     recv_a,
     send_b,
     recv_b,
-    send_h,
-    recv_h,
     list_sem,
 ):
     peers, az_size = lax.axis_size("date"), lax.axis_size("az")
@@ -280,6 +290,7 @@
     width = slc_ref.shape[3] // peers
     images_dev = 2 * date_dev
     sides = ((-1, az > 0), (1, az < az_size - 1))
+    kinds = ((0, None),) + sides
 
     named = pltpu.make_async_copy(pairs_hbm, pairs_ref, pairs_sem)
     barrier = pltpu.get_barrier_semaphore()
@@ -307,7 +318,7 @@
     pl.semaphore_wait(barrier, greeted)
 
     def images(o):
-        peer = lax.rem(me + o, peers)
+        peer = partner(me, o)
         return pltpu.make_async_remote_copy(
             src_ref=sent.at[peer],
             dst_ref=held.at[me],
@@ -317,7 +328,7 @@
             device_id_type=MESH,
         )
 
-    for o in range(1, peers):
+    for o in range(peers - 1, 0, -1):
         images(o).start()
     named.wait()
     for r in range(rounds):
@@ -354,91 +365,101 @@
         chosen[r, 128:, :] = powers.T.astype(jnp.bfloat16)
     for o in range(1, peers):
         images(o).wait_recv()
-        owner = lax.rem(me + peers - o, peers)
+        owner = partner(me, o)
         take(owner, held[owner])
 
-    def results(o):
-        peer = lax.rem(me + o, peers)
+    def result(kind, peer):
+        step, _ = kinds[kind]
+        device = {"date": peer}
+        if step:
+            device["az"] = az + step
         return pltpu.make_async_remote_copy(
-            src_ref=sums.at[peer],
-            dst_ref=tiles.at[me],
-            send_sem=send_b,
-            recv_sem=recv_b,
-            device_id={"date": peer},
+            src_ref=(near_sums.at[kind - 1] if kind else sums).at[peer],
+            dst_ref=(near_tiles.at[kind - 1] if kind else tiles).at[me],
+            send_sem=send_b.at[kind],
+            recv_sem=recv_b.at[kind],
+            device_id=device,
             device_id_type=MESH,
         )
 
-    def serve(o, carry):
-        peer = lax.rem(me + o, peers)
+    def serve(n, carry):
+        m = peers - 1 - n
+        peer = partner(me, m)
+        shares = []
         for r in range(rounds):
             real, imag = [], []
             for k in range(peers):
                 date = ids[r * peers + k, peer]
                 real.append(full[2 * date])
                 imag.append(full[2 * date + 1])
-            sums[peer, r] = cell_sums(real, imag)
-
-        @pl.when(o < peers)
-        def _():
-            results(o).start()
+            shares.append(shares_of(cell_sums(real, imag)))
+        for kind in range(3):
+            share = jnp.concatenate([shares[r][kind] for r in range(rounds)], 0)
+            if kind:
+                near_sums[kind - 1, peer] = share.astype(jnp.bfloat16)
+            else:
+                sums[peer] = share
+        for kind, (step, there) in enumerate(kinds):
+
+            @pl.when(there if step else m > 0)
+            def _():
+                result(kind, peer).start()
 
         return carry
 
-    lax.fori_loop(1, peers + 1, serve, 0)
+    for kind, (step, there) in enumerate(kinds):
+        if step:
+
+            @pl.when(jnp.logical_not(there))
+            def _():
+                near_tiles[2 - kind] = jnp.zeros_like(near_tiles[2 - kind])
+
+    lax.fori_loop(0, peers, serve, 0)
     tiles[me] = sums[me]
-    others = pl.ds(0, peers - 1)
-
-    def all_of(src, dst, send_sem, recv_sem):
+
+    def all_of(src, dst, count, send_sem, recv_sem):
+        part = pl.ds(0, count)
         return pltpu.make_async_remote_copy(
-            src_ref=src.at[others],
-            dst_ref=dst.at[others],
+            src_ref=src.at[part],
+            dst_ref=dst.at[part],
             send_sem=send_sem,
             recv_sem=recv_sem,
             device_id={"date": lax.rem(me + 1, peers)},
             device_id_type=MESH,
         )
 
-    all_of(sums, tiles, send_b, recv_b).wait_recv()
+    def all_results(kind):
+        sems = send_b.at[kind], recv_b.at[kind]
+        if kind:
+            return all_of(near_sums.at[kind - 1], near_tiles.at[kind - 1], peers, *sems)
+        return all_of(sums, tiles, peers - 1, *sems)
+
+    all_results(0).wait_recv()
+    for kind, (step, there) in enumerate(kinds):
+        if step:
+
+            @pl.when(there)
+            def _():
+                all_results(3 - kind).wait_recv()
+
+    own, near = [], []
+    for j in range(peers):
+        own.append(tiles[j])
+        sides_sum = near_tiles[0, j].astype(jnp.float32) + near_tiles[1, j].astype(jnp.float32)
+        near.append(both_rows(own[-1]) + sides_sum)
     for r in range(rounds):
-        for k, tile in enumerate(table_of([tiles[j, r] for j in range(peers)])):
-            table[r, 8 * k : 8 * k + 8, :] = tile
-
-    def edge(n, step):
-        return pltpu.make_async_remote_copy(
-            src_ref=table,
-            dst_ref=halo.at[n],
-            send_sem=send_h.at[n],
-            recv_sem=recv_h.at[n],
-            device_id={"az": az + step},
-            device_id_type=MESH,
-        )
-
-    for n, (step, there) in enumerate(sides):
-
-        @pl.when(there)
-        def _():
-            edge(n, step).start()
-
-        @pl.when(jnp.logical_not(there))
-        def _():
-            halo[1 - n] = jnp.zeros_like(halo[1 - n])
-
-    for n, (step, there) in enumerate(sides):
-
-        @pl.when(there)
-        def _():
-            edge(1 - n, step).wait_recv()
-
-    for r in range(rounds):
-        boxed_ref[r] = box_of(table[r], halo[1, r], halo[0, r])
-
-    all_of(sent, held, send_a, recv_a.at[0]).wait_send()
-    all_of(sums, tiles, send_b, recv_b).wait_send()
-    for n, (step, there) in enumerate(sides):
-
-        @pl.when(there)
-        def _():
-            edge(n, step).wait_send()
+        at = slice(8 * r, 8 * r + 8)
+        table[r] = jnp.concatenate(table_of([x[at] for x in own]), 0)
+        boxed_ref[r] = box_of(jnp.concatenate(table_of([x[at] for x in near]), 0))
+
+    all_of(sent, held, peers - 1, send_a, recv_a.at[0]).wait_send()
+    all_results(0).wait_send()
+    for kind, (step, there) in enumerate(kinds):
+        if step:
+
+            @pl.when(there)
+            def _():
+                all_results(kind).wait_send()
 
 
 def pairs_kernel(table_ref, boxed_ref, chosen_ref, ifg_hbm, coh_hbm, ifg_ref, coh_ref, sems):
@@ -451,7 +472,7 @@
 
     for r in range(rounds):
         means = jnp.dot(
-            chosen_ref[r, :128, :], in_three(table_ref[r]), preferred_element_type=jnp.float32
+            chosen_ref[r, :128], in_two(table_ref[r]), preferred_element_type=jnp.float32
         )
         for c in range(2):
             for row in range(2):
@@ -459,7 +480,7 @@
                 ifg_ref[pl.ds(256 * r + 2 * c + row, 64, stride=4), :] = part
         out(r, ifg_ref, ifg_hbm, 0).start()
         parts = jnp.dot(
-            chosen_ref[r], in_three(boxed_ref[r]), preferred_element_type=jnp.float32
+            chosen_ref[r], in_two(boxed_ref[r]), preferred_element_type=jnp.float32
         )
         size = jnp.sqrt(parts[:64] * parts[:64] + parts[64:128] * parts[64:128])
         coherence = size / jnp.sqrt(parts[128:192] * parts[192:])
@@ -488,7 +509,7 @@
         out_shape=(
             jax.ShapeDtypeStruct((rounds, 64, 128), jnp.float32),
             jax.ShapeDtypeStruct((rounds, 64, 128), jnp.float32),
-            jax.ShapeDtypeStruct((rounds, 256, 192), jnp.bfloat16),
+            jax.ShapeDtypeStruct((rounds, 256, 128), jnp.bfloat16),
         ),
         in_specs=[hbm, hbm],
         out_specs=(vmem,) * 3,
@@ -497,9 +518,10 @@
             pltpu.VMEM((peers, rows, width), jnp.bfloat16),
             pltpu.VMEM((peers, rows, width), jnp.bfloat16),
             pltpu.VMEM((peers * date_dev * 2, lines, width), jnp.float32),
-            pltpu.VMEM((peers, rounds, 8, 128), jnp.float32),
-            pltpu.VMEM((peers, rounds, 8, 128), jnp.float32),
-            pltpu.VMEM((2, rounds, 64, 128), jnp.float32),
+            pltpu.VMEM((peers, rounds * 8, 128), jnp.float32),
+            pltpu.VMEM((peers, rounds * 8, 128), jnp.float32),
+            pltpu.VMEM((2, peers, rounds * 8, 128), jnp.bfloat16),
+            pltpu.VMEM((2, peers, rounds * 8, 128), jnp.bfloat16),
             pltpu.VMEM((rounds * peers, 128), jnp.int32),
             pltpu.SMEM((rounds * peers, 128), jnp.int32),
             pltpu.VMEM((rounds, 2, pairs.shape[1]), jnp.int32),
@@ -507,10 +529,8 @@
             dma,
             dma,
             dma((peers,)),
-            dma,
-            dma,
-            dma((2,)),
-            dma((2,)),
+            dma((3,)),
+            dma((3,)),
             dma,
         ],
         compiler_params=pltpu.CompilerParams(

time: 22.7 us -> 20 us (0.88)
  Pallas kernels: 21.9 us -> 19.2 us
    pallas_call x1, Pallas kernels: 20.8 us -> 18.1 us  [per_device_few(): pl.pallas_call(stack_kernel, out_shape=(jax.ShapeDtypeStruct((rounds, 64,...]
where the time goes in v2:
time: 20 us; the launch traced here: 19.8 us
  Pallas kernels  19.2 us (96%)
  between operations  0.64 us (3%)
    pallas_call x1, Pallas kernels, per_device_few(): pl.pallas_call(stack_kernel, out_shape=(jax.ShapeDtypeStruct((rounds, 64,...  18.1 us
    pallas_call x1, Pallas kernels, per_device_few(): pl.pallas_call(pairs_kernel, out_shape=(jax.ShapeDtypeStruct(ifg_shape, j...  1.02 us

profile of v2, /device:TPU:1, one launch (start us, length us, event | category | flops | bytes accessed | tf_op | source)
XLA Modules:
  0.0 19.8 jit_solution(13525502635148001223)
XLA Ops:
  0.6 18.1 %shard_map.41 = (f32[2,64,128]{2,1,0:T(8,128)S(1)}, f32[2,64,128]{2,1,0:T(8,128)S(1)}, bf16[2,256,128]{2,1,0:T(8,128)(2,1)S(1)}) custom-call(f32[6,2,8,1024]{3,2,1,0:T(8,128)} %slc_ref.1, s32[2,2,512]{2,1,0:T(2,128)} %bitcast.3), custom_call_target="tpu_custom_call" | custom-call | tf_op jit(solution)/shard_map/pallas_call | solution.py:507
  18.8 1.0 %shard_map.42 = (f32[512,64]{1,0:T(8,128)}, f32[256,64]{1,0:T(8,128)}) custom-call(f32[2,64,128]{2,1,0:T(8,128)S(1)} %get-tuple-element.7.table_ref, f32[2,64,128]{2,1,0:T(8,128)S(1)} %get-tuple-element.8.boxed_ref, bf16[2,256,128]{2,1,0:T(8,128)(2,1)S(1)} %get-tuple-element.9.chosen_ref), custom_call_target="tpu_custom_call" | custom-call | tf_op jit(solution)/shard_map/pallas_call | solution.py:545

commit v3 on v2

--- a/solution.py
+++ b/solution.py
@@ -282,6 +282,7 @@
     send_b,
     recv_b,
     list_sem,
+    known,
 ):
     peers, az_size = lax.axis_size("date"), lax.axis_size("az")
     me, az = lax.axis_index("date"), lax.axis_index("az")
@@ -297,10 +298,22 @@
     for n in range(date_dev):
         pltpu.make_async_copy(slc_ref.at[n], lines.at[n], line_sem).start()
     named.start()
-    for o in range(1, peers):
-        pl.semaphore_signal(
-            barrier, inc=1, device_id={"date": lax.rem(me + o, peers)}, device_id_type=MESH
-        )
+    across = lax.rem(me, 2)
+    along = me // 2
+    depth = peers // 2
+    beside = me + 1 - 2 * across
+
+    def greet(sem):
+        pl.semaphore_signal(sem, inc=1, device_id={"date": beside}, device_id_type=MESH)
+        for step, there in ((-1, along > 0), (1, along < depth - 1)):
+
+            @pl.when(there)
+            def _():
+                pl.semaphore_signal(
+                    sem, inc=1, device_id={"date": me + 2 * step}, device_id_type=MESH
+                )
+
+    greet(barrier)
     for step, there in sides:
 
         @pl.when(there)
@@ -314,22 +327,49 @@
             part = lines[n, :, :, j * width : (j + 1) * width]
             at = slice(n * rows_date, (n + 1) * rows_date)
             sent[j, at] = part.reshape(rows_date, width).astype(jnp.bfloat16)
-    greeted = peers - 1 + (az > 0).astype(jnp.int32) + (az < az_size - 1).astype(jnp.int32)
-    pl.semaphore_wait(barrier, greeted)
-
-    def images(o):
-        peer = partner(me, o)
+    close = 1 + (along > 0).astype(jnp.int32) + (along < depth - 1).astype(jnp.int32)
+    lines_near = (az > 0).astype(jnp.int32) + (az < az_size - 1).astype(jnp.int32)
+    pl.semaphore_wait(barrier, close + lines_near)
+
+    def images(peer):
         return pltpu.make_async_remote_copy(
             src_ref=sent.at[peer],
             dst_ref=held.at[me],
             send_sem=send_a,
-            recv_sem=recv_a.at[o],
+            recv_sem=recv_a.at[me],
             device_id={"date": peer},
             device_id_type=MESH,
         )
 
-    for o in range(peers - 1, 0, -1):
-        images(o).start()
+    def tell(sem, step, there):
+        @pl.when(there)
+        def _():
+            pl.semaphore_signal(
+                sem, inc=1, device_id={"date": me + 2 * step}, device_id_type=MESH
+            )
+
+    def send(column, step):
+        @pl.when((along + step >= 0) & (along + step < depth))
+        def _():
+            images(column + 2 * step).start()
+
+    for way in (-1, 1):
+        tell(known.at[(way + 1) // 2, 0], way, (along + way >= 0) & (along + way < depth))
+    for way in (1, -1):
+        send(me, way)
+    images(beside).start()
+    for hops in range(1, depth):
+        for way in (1, -1):
+            news = known.at[(way + 1) // 2]
+
+            @pl.when((along - way * hops >= 0) & (along - way * hops < depth))
+            def _():
+                pl.semaphore_wait(news.at[hops - 1], 1)
+                if hops < depth - 1:
+                    tell(news.at[hops], way, (along + way >= 0) & (along + way < depth))
+                send(me, -way * (hops + 1))
+                send(beside, -way * hops)
+
     named.wait()
     for r in range(rounds):
         listed[r * peers : (r + 1) * peers, :] = list_dates(
@@ -363,9 +403,19 @@
         products, powers = picks(*ranks, peers)
         chosen[r, :128, :] = products.T.astype(jnp.bfloat16)
         chosen[r, 128:, :] = powers.T.astype(jnp.bfloat16)
+    def arrival(owner):
+        return pltpu.make_async_remote_copy(
+            src_ref=sent.at[owner],
+            dst_ref=held.at[owner],
+            send_sem=send_a,
+            recv_sem=recv_a.at[owner],
+            device_id={"date": owner},
+            device_id_type=MESH,
+        )
+
     for o in range(1, peers):
-        images(o).wait_recv()
         owner = partner(me, o)
+        arrival(owner).wait_recv()
         take(owner, held[owner])
 
     def result(kind, peer):
@@ -382,9 +432,7 @@
             device_id_type=MESH,
         )
 
-    def serve(n, carry):
-        m = peers - 1 - n
-        peer = partner(me, m)
+    def serve(peer, carry):
         shares = []
         for r in range(rounds):
             real, imag = [], []
@@ -401,7 +449,7 @@
                 sums[peer] = share
         for kind, (step, there) in enumerate(kinds):
 
-            @pl.when(there if step else m > 0)
+            @pl.when(there if step else peer != me)
             def _():
                 result(kind, peer).start()
 
@@ -532,6 +580,7 @@
             dma((3,)),
             dma((3,)),
             dma,
+            pltpu.SemaphoreType.REGULAR((2, peers // 2 - 1)),
         ],
         compiler_params=pltpu.CompilerParams(
             collective_id=0, has_side_effects=True, vmem_limit_bytes=VMEM_LIMIT

time: 20 us -> 19.3 us (0.965)
  Pallas kernels: 19.2 us -> 18.4 us
    pallas_call x1, Pallas kernels: 18.1 us -> 17.4 us  [per_device_few(): pl.pallas_call(stack_kernel, out_shape=(jax.ShapeDtypeStruct((rounds, 64,...]
where the time goes in v3:
time: 19.3 us; the launch traced here: 19.1 us
  Pallas kernels  18.4 us (95%)
  between operations  0.64 us (3%)
    pallas_call x1, Pallas kernels, per_device_few(): pl.pallas_call(stack_kernel, out_shape=(jax.ShapeDtypeStruct((rounds, 64,...  17.4 us
    pallas_call x1, Pallas kernels, per_device_few(): pl.pallas_call(pairs_kernel, out_shape=(jax.ShapeDtypeStruct(ifg_shape, j...  1.02 us

profile of v3, /device:TPU:1, one launch (start us, length us, event | category | flops | bytes accessed | tf_op | source)
XLA Modules:
  0.0 19.1 jit_solution(1107487825369767655)
XLA Ops:
  0.6 17.4 %shard_map.41 = (f32[2,64,128]{2,1,0:T(8,128)S(1)}, f32[2,64,128]{2,1,0:T(8,128)S(1)}, bf16[2,256,128]{2,1,0:T(8,128)(2,1)S(1)}) custom-call(f32[6,2,8,1024]{3,2,1,0:T(8,128)} %slc_ref.1, s32[2,2,512]{2,1,0:T(2,128)} %bitcast.3), custom_call_target="tpu_custom_call" | custom-call | tf_op jit(solution)/shard_map/pallas_call | solution.py:555
  18.1 1.0 %shard_map.42 = (f32[512,64]{1,0:T(8,128)}, f32[256,64]{1,0:T(8,128)}) custom-call(f32[2,64,128]{2,1,0:T(8,128)S(1)} %get-tuple-element.7.table_ref, f32[2,64,128]{2,1,0:T(8,128)S(1)} %get-tuple-element.8.boxed_ref, bf16[2,256,128]{2,1,0:T(8,128)(2,1)S(1)} %get-tuple-element.9.chosen_ref), custom_call_target="tpu_custom_call" | custom-call | tf_op jit(solution)/shard_map/pallas_call | solution.py:594

commit v4 on v2

--- a/solution.py
+++ b/solution.py
@@ -6,6 +6,7 @@
 from jax.sharding import PartitionSpec as P
 
 CAP = 2
+FAR_FIRST = (7, 5, 6, 3, 4, 2, 1)
 VMEM_LIMIT = 4 << 20
 
 
@@ -328,7 +329,7 @@
             device_id_type=MESH,
         )
 
-    for o in range(peers - 1, 0, -1):
+    for o in FAR_FIRST:
         images(o).start()
     named.wait()
     for r in range(rounds):
@@ -382,9 +383,7 @@
             device_id_type=MESH,
         )
 
-    def serve(n, carry):
-        m = peers - 1 - n
-        peer = partner(me, m)
+    def serve(peer, carry):
         shares = []
         for r in range(rounds):
             real, imag = [], []
@@ -401,7 +400,7 @@
                 sums[peer] = share
         for kind, (step, there) in enumerate(kinds):
 
-            @pl.when(there if step else m > 0)
+            @pl.when(there if step else peer != me)
             def _():
                 result(kind, peer).start()
 

time: 20 us -> 19 us (0.950)
  Pallas kernels: 19.2 us -> 18.2 us
    pallas_call x1, Pallas kernels: 18.1 us -> 17.2 us  [per_device_few(): pl.pallas_call(stack_kernel, out_shape=(jax.ShapeDtypeStruct((rounds, 64,...]
where the time goes in v4:
time: 19 us; the launch traced here: 18.9 us
  Pallas kernels  18.2 us (96%)
  between operations  0.64 us (3%)
    pallas_call x1, Pallas kernels, per_device_few(): pl.pallas_call(stack_kernel, out_shape=(jax.ShapeDtypeStruct((rounds, 64,...  17.2 us
    pallas_call x1, Pallas kernels, per_device_few(): pl.pallas_call(pairs_kernel, out_shape=(jax.ShapeDtypeStruct(ifg_shape, j...  1.02 us

profile of v4, /device:TPU:1, one launch (start us, length us, event | category | flops | bytes accessed | tf_op | source)
XLA Modules:
  0.0 18.9 jit_solution(1467814431718535703)
XLA Ops:
  0.6 17.2 %shard_map.41 = (f32[2,64,128]{2,1,0:T(8,128)S(1)}, f32[2,64,128]{2,1,0:T(8,128)S(1)}, bf16[2,256,128]{2,1,0:T(8,128)(2,1)S(1)}) custom-call(f32[6,2,8,1024]{3,2,1,0:T(8,128)} %slc_ref.1, s32[2,2,512]{2,1,0:T(2,128)} %bitcast.3), custom_call_target="tpu_custom_call" | custom-call | tf_op jit(solution)/shard_map/pallas_call | solution.py:506
  17.9 1.0 %shard_map.42 = (f32[512,64]{1,0:T(8,128)}, f32[256,64]{1,0:T(8,128)}) custom-call(f32[2,64,128]{2,1,0:T(8,128)S(1)} %get-tuple-element.7.table_ref, f32[2,64,128]{2,1,0:T(8,128)S(1)} %get-tuple-element.8.boxed_ref, bf16[2,256,128]{2,1,0:T(8,128)(2,1)S(1)} %get-tuple-element.9.chosen_ref), custom_call_target="tpu_custom_call" | custom-call | tf_op jit(solution)/shard_map/pallas_call | solution.py:544

commit v5 on v4

--- a/solution.py
+++ b/solution.py
@@ -103,7 +103,7 @@
 
 
 LINES, SAMPLES = 4, 16
-STEPS = ((0, 2, 2), (0, 2, 1), (1, 8, 8), (1, 8, 4), (1, 8, 2), (1, 8, 1))
+STEPS = ((1, 8, 1), (1, 8, 2), (1, 8, 4), (1, 8, 8), (0, 2, 1), (0, 2, 2))
 
 
 def iota(shape, dim):
@@ -112,45 +112,56 @@
 
 def place_of(leaf):
     bit = [(leaf >> n) & 1 for n in range(6)]
-    return 32 * bit[3] + 16 * bit[4] + 8 * bit[5] + 4 * bit[0] + 2 * bit[1] + bit[2]
+    return 32 * bit[2] + 16 * bit[1] + 8 * bit[0] + 4 * bit[5] + 2 * bit[4] + bit[3]
 
 
 def rolled(x, shift, dim):
     return pltpu.roll(x, shift % x.shape[dim], dim)
 
 
-def join(one, two, dim, unit, dist, phase):
-    low = ((iota(one.shape, dim) - unit * phase) & (unit * dist)) == 0
+def lower(shape, dim, far):
+    return (iota(shape, dim) & far) == 0
+
+
+def join(one, two, dim, far):
+    low = lower(one.shape, dim, far)
     kept = jnp.where(low, one, two)
     other = jnp.where(low, two, one)
-    return kept + rolled(other, -unit * dist, dim)
+    return kept + rolled(other, -far, dim)
 
 
 def cell_sums(real, imag):
     count = len(real)
     couples = [(i, j) for i in range(count) for j in range(i + 1, count)]
-
-    def quantity(place):
-        if place < len(couples):
-            i, j = couples[place]
-            return real[i] * real[j] + imag[i] * imag[j]
-        place -= len(couples)
-        if place < len(couples):
-            i, j = couples[place]
-            return imag[i] * real[j] - real[i] * imag[j]
-        i = place - len(couples)
+    dim, unit, dist = STEPS[0]
+    low = lower(real[0].shape, dim, unit * dist)
+    mixed = []
+    for re, im in zip(real, imag):
+        kept = (jnp.where(low, re, im), jnp.where(low, im, -re))
+        other = (jnp.where(low, im, re), jnp.where(low, -re, im))
+        mixed.append((kept, other))
+
+    def power(i):
         return real[i] * real[i] + imag[i] * imag[i]
 
-    def build(level, base, phases):
-        if level == 0:
-            return quantity(place_of(base))
+    def first(place):
+        n = (place & 7) + (place >> 4 << 3)
+        if n >= len(couples):
+            i = n - len(couples)
+            return join(power(i), power(i + count // 2), dim, unit * dist)
+        i, j = couples[n]
+        kept, other = [a * real[j] + b * imag[j] for a, b in mixed[i]]
+        return kept + rolled(other, -unit * dist, dim)
+
+    def build(level, base):
+        if level == 1:
+            return first(place_of(base))
         dim, unit, dist = STEPS[level - 1]
-        moved = tuple(p + dist if d == dim else p for d, p in enumerate(phases))
-        one = build(level - 1, base, phases)
-        two = build(level - 1, base + (1 << (level - 1)), moved)
-        return join(one, two, dim, unit, dist, phases[dim])
-
-    return build(len(STEPS), 0, (0, 0))
+        one = build(level - 1, base)
+        two = build(level - 1, base + (1 << (level - 1)))
+        return join(one, two, dim, unit * dist)
+
+    return build(len(STEPS), 0)
 
 
 def in_two(x):
@@ -209,14 +220,20 @@
     return jnp.where(iota((128, 128), 0) & 63 == places, values, 0.0)
 
 
+def spot(n):
+    return (n & 7) + (n >> 3 << 4)
+
+
 def picks(rank_a, rank_b, count):
     first = iota(rank_a.shape, 1) < 64
     low, high = jnp.minimum(rank_a, rank_b), jnp.maximum(rank_a, rank_b)
-    couples = count * (count - 1) // 2
     place = ((low * (2 * count - 1 - low)) >> 1) + high - low - 1
     sign = jnp.where(first | (rank_a < rank_b), 1.0, -1.0)
-    products = pick(place + jnp.where(first, 0, couples), sign)
-    powers = pick(2 * couples + jnp.where(first, rank_a, rank_b), jnp.ones_like(sign))
+    products = pick(spot(place) + jnp.where(first, 0, 8), sign)
+    rank = jnp.where(first, rank_a, rank_b)
+    half = count // 2
+    place = spot(count * (count - 1) // 2 + (rank & (half - 1)))
+    powers = pick(place + jnp.where(rank < half, 0, 8), jnp.ones_like(sign))
     return products, powers
 
 

time: 19 us -> 19 us (level)
  no operation moved by 1% of the time
where the time goes in v5:
time: 19 us; the launch traced here: 18.8 us
  Pallas kernels  18.2 us (96%)
  between operations  0.64 us (3%)
    pallas_call x1, Pallas kernels, per_device_few(): pl.pallas_call(stack_kernel, out_shape=(jax.ShapeDtypeStruct((rounds, 64,...  17.2 us
    pallas_call x1, Pallas kernels, per_device_few(): pl.pallas_call(pairs_kernel, out_shape=(jax.ShapeDtypeStruct(ifg_shape, j...  1.02 us

profile of v5, /device:TPU:1, one launch (start us, length us, event | category | flops | bytes accessed | tf_op | source)
XLA Modules:
  0.0 18.8 jit_solution(9200071412918706010)
XLA Ops:
  0.6 17.2 %shard_map.41 = (f32[2,64,128]{2,1,0:T(8,128)S(1)}, f32[2,64,128]{2,1,0:T(8,128)S(1)}, bf16[2,256,128]{2,1,0:T(8,128)(2,1)S(1)}) custom-call(f32[6,2,8,1024]{3,2,1,0:T(8,128)} %slc_ref.1, s32[2,2,512]{2,1,0:T(2,128)} %bitcast.3), custom_call_target="tpu_custom_call" | custom-call | tf_op jit(solution)/shard_map/pallas_call | solution.py:523
  17.8 1.0 %shard_map.42 = (f32[512,64]{1,0:T(8,128)}, f32[256,64]{1,0:T(8,128)}) custom-call(f32[2,64,128]{2,1,0:T(8,128)S(1)} %get-tuple-element.7.table_ref, f32[2,64,128]{2,1,0:T(8,128)S(1)} %get-tuple-element.8.boxed_ref, bf16[2,256,128]{2,1,0:T(8,128)(2,1)S(1)} %get-tuple-element.9.chosen_ref), custom_call_target="tpu_custom_call" | custom-call | tf_op jit(solution)/shard_map/pallas_call | solution.py:561
